TPU v7x, 256 devices: a whole 4x4x8 slice. The times are simulated.
256 devices in a mesh: cube: 4 (over y), row: 4 (over x), col: 16 (over z, core).
Axes of the slice: x: 4, y: 4, z: 8, core: 2. Of those that a mesh axis runs over, the one named last changes fastest.
Arguments:
- front_entries: float32 [4, 8192, 8192], P('cube', 'row', 'col'), as said below
- child_updates: float32 [4, 2, 4096, 4096], P('cube', None, ('row', 'col')), may hold values from -6 to 6, as said below
- child_index: int32 [4, 2, 64], replicated, may hold values from 0 to 127, as said below
- child_blocks: int32 [4, 2], replicated, may hold values from 32 to 64
Outputs:
- factored: float32 [4, 8192, 8192], P('cube', 'row', 'col')
Inputs may be any that keep to these rules, and one draw needn't show every extreme that they name: `front_entries`: each front is symmetric positive definite in natural numbering. `child_updates`: each contribution block is symmetric. `child_index`: each list names 64 different front blocks; entry t of a list names a front block whose rows lie in a 512-wide block b of front variables with b mod 4 = t div (16).
All inputs are finite; a program needn't handle non-finite values.
Results may differ from a plain program's by a relative error of at most 0.0001.
Values sent between devices are 32-bit elements; how exact they have to be, the bound alone decides.
No kernel may reach another device: no remote copies, remote signals or barrier semaphores. Data moves between devices by JAX's collectives and lax.ppermute only.
A program may use at most 128 MiB of HBM per device.

v0:
```python
import jax
import jax.numpy as jnp
from jax import lax
from jax.sharding import PartitionSpec as P

F = 8192
B = 512
SBLK = 64
CR = 4096
PANELS = 2
HIGHEST_PRECISION = lax.Precision.HIGHEST


def swapped(value, axis, apart):
    mask = 2**apart
    pairs = [(source, source ^ mask) for source in range(lax.axis_size(axis))]
    return lax.ppermute(value, axis, pairs)


def spread_2(block, axis, holder):
    block = jnp.where(lax.axis_index(axis) == holder, block, jnp.zeros_like(block))
    return lax.psum(block, axis)


def storage_position(variable, parts, local_size):
    block = variable // B
    return block % parts * local_size + block // parts * B + variable % B


def natural_variable(local_size, parts, index):
    local = jnp.arange(local_size, dtype=jnp.int32)
    return (local // B * parts + index) * B + local % B


def child_variable(block_lists, offsets):
    return jnp.take(block_lists, offsets // SBLK, axis=1) * SBLK + offsets % SBLK


def solve_panel(rows_in, factor, row_block, panel_step, row_index, root_row, row_slot):
    solved = lax.linalg.triangular_solve(
        factor, rows_in, left_side=False, lower=True, transpose_a=True
    )
    solved = jnp.where((row_block < panel_step)[:, None], 0.0, solved)
    with_pivot = lax.dynamic_update_slice(solved, factor, (row_slot * B, 0))
    return jnp.where(row_index == root_row, with_pivot, solved)


def on_device(front_entries, child_updates, child_index, child_blocks):
    n_row = lax.axis_size("row")
    n_col = lax.axis_size("col")
    row_index = lax.axis_index("row")
    col_index = lax.axis_index("col")
    cube_index = lax.axis_index("cube")
    sibling = jnp.bitwise_xor(cube_index, 1)
    working = front_entries[0]
    rows_here, cols_here = working.shape
    piece_rows = child_updates.shape[2]
    arrived_child = swapped(child_updates[0, 1], "cube", 0)
    pieces = jnp.stack([child_updates[0, 0], arrived_child])
    block_lists = jnp.stack([child_index[cube_index, 0], child_index[sibling, 1]])
    counts = jnp.stack([child_blocks[cube_index, 0], child_blocks[sibling, 1]])
    offsets = jnp.arange(CR, dtype=jnp.int32)
    flat_index = row_index * n_col + col_index
    own_rows = flat_index * piece_rows + jnp.arange(piece_rows, dtype=jnp.int32)
    live_cols = (offsets // SBLK)[None, :] < counts[:, None]
    live_rows = (own_rows // SBLK)[None, :] < counts[:, None]
    values = jnp.where(live_rows[:, :, None] & live_cols[:, None, :], pieces, 0.0)
    col_targets = storage_position(child_variable(block_lists, offsets), n_col, cols_here)

    def widen(child_values, targets):
        return jnp.zeros((piece_rows, F), jnp.float32).at[:, targets].add(child_values)

    spread = jax.vmap(widen)(values, col_targets).reshape(2 * piece_rows, F)
    arrived = lax.all_to_all(spread, "col", split_axis=1, concat_axis=0, tiled=True)
    sources = jnp.arange(n_col, dtype=jnp.int32)
    source_rows = (row_index * n_col + sources)[:, None] * piece_rows + jnp.arange(
        piece_rows, dtype=jnp.int32
    )[None, :]
    natural_rows = child_variable(block_lists, source_rows)
    row_targets = storage_position(jnp.swapaxes(natural_rows, 0, 1), n_row, rows_here).reshape(-1)
    local_rows = row_targets - row_index * rows_here
    working = working.at[local_rows].add(arrived)
    row_block = natural_variable(rows_here, n_row, row_index) // B
    col_block = natural_variable(cols_here, n_col, col_index) // B
    identity = jnp.eye(B, dtype=jnp.float32)
    for panel_step in range(PANELS):
        root_row = panel_step % n_row
        row_slot = panel_step // n_row
        root_col = panel_step % n_col
        col_slot = panel_step // n_col
        diagonal = working[row_slot * B : (row_slot + 1) * B, col_slot * B : (col_slot + 1) * B]
        panel_cols = working
        own_pivot = jnp.where(col_index == root_col, diagonal, identity)
        pivot_block = spread_2(own_pivot, "row", root_row)
        factor = jnp.linalg.cholesky(pivot_block)
        own_lower = solve_panel(
            panel_cols, factor, row_block, panel_step, row_index, root_row, row_slot
        )
        lower_rows = spread_2(own_lower, "col", root_col)
        global_block = 0 + col_index
        block_piece = lax.dynamic_slice_in_dim(lower_rows, global_block // n_row * B, B, 0)
        col_pieces = jnp.where(global_block % n_row == row_index, block_piece, 0.0)
        lower_cols = lax.psum(col_pieces, "row")
        working = working - jnp.dot(
            lower_rows,
            lower_cols.T,
            precision=HIGHEST_PRECISION,
            preferred_element_type=jnp.float32,
        )
        replaced = working.at[:, col_slot * B : (col_slot + 1) * B].set(lower_rows)
        working = jnp.where(col_index == root_col, replaced, working)
    finished = (row_block < PANELS)[:, None] & (col_block >= PANELS)[None, :]
    return jnp.where(finished, 0.0, working)[None]


def solution(mesh):
    in_specs = (P("cube", "row", "col"), P("cube", None, ("row", "col"), None), P(), P())
    out_specs = P("cube", "row", "col")
    return jax.shard_map(
        on_device, mesh=mesh, in_specs=in_specs, out_specs=out_specs, check_vma=False
    )
```

profile of v0, /device:TPU:8, one launch (start us, length us, event | category | flops | bytes accessed | tf_op | source)
XLA Modules:
  0.0 1050.2 jit_solution(9398155492795176346)
XLA Ops:
  6.5 4.8 copy.227
  16.2 14.1 %gather_fusion.1 = s32[4096,2]{1,0:T(8,128)} fusion(s32[2,64]{0,1:T(8,128)S(1)} %copy.127, s32[4096]{0:T(1024)S(1)} %broadcast_clamp_fusion), kind=kCustom, calls=%fused_computation.1 | custom fusion | bytes 81920 | tf_op jit(solution)/shard_map/jit(_take)/gather | solution.py:36
  30.3 7.2 compare_select_fusion
  42.0 2.6 broadcast_select_fusion.2
  48.5 2.7 copy.174
  51.3 48.2 %scatter_custom_fusion.1 = f32[16384,64]{1,0:T(8,128)} fusion(s32[8192]{0:T(1024)S(1)} %bitcast.172, f32[8192,64]{1,0:T(8,128)} %bitcast.167, f32[]{:T(128)} %constant.447.clone.1), kind=kCustom, calls=%fused_computation.11 | custom fusion | flops 524288 | bytes 4194816
  99.5 8.7 copy.175
  108.1 4.6 copy.137
  112.8 3.3 copy.182
  116.0 4.4 copy.138
  120.4 6.9 all-to-all-start
  127.6 2.8 gather_fusion
  131.0 90.6 %all-to-all-done = f32[128,16,512]{2,0,1:T(8,128)} async-done(((f32[128,16,512]{2,0,1:T(8,128)}), f32[128,16,512]{2,0,1:T(8,128)}, u32[]{:S(2)}, u32[]{:S(2)}) %all-to-all-start) | async-done | bytes 4194336 | tf_op jit(solution)/shard_map/all_to_all | solution.py:74
  221.6 17.4 %scatter_fusion = f32[2048,512]{1,0:T(8,128)} fusion(f32[2048,512]{1,0:T(8,128)} %bitcast.156, s32[2048]{0:T(1024)S(1)} %bitcast.171, f32[2048,512]{1,0:T(8,128)} %bitcast.19), kind=kCustom, calls=%fused_computation.2 | custom fusion | flops 1048576 | bytes 12591104 | tf_op jit(solution)/shard_map/scatter-add | solution.py:82
  239.0 5.4 copy.139
  247.3 50.5 %all-reduce.8.cloned.1.call-done = f32[512,512]{0,1:T(8,128)} async-done(((f32[512,512]{0,1:T(8,128)}), f32[512,512]{0,1:T(8,128)}) %all-reduce.8.cloned.1.call-update) | async-done | bytes 1048592 | tf_op jit(solution)/shard_map/psum | solution.py:22
  300.8 11.7 %cholesky.286 = f32[128,128]{1,0:T(8,128)S(1)} custom-call(f32[128,128]{1,0:T(8,128)S(1)} %cholesky.426), custom_call_target="Cholesky" | custom-call | tf_op jit(solution)/shard_map/jit(cholesky)/cholesky | solution.py:95
  312.5 9.8 custom-call.27
  323.0 11.7 %cholesky.305 = f32[128,128]{1,0:T(8,128)S(1)} custom-call(f32[128,128]{1,0:T(8,128)S(1)} %cholesky.430), custom_call_target="Cholesky" | custom-call | tf_op jit(solution)/shard_map/jit(cholesky)/cholesky | solution.py:95
  335.1 9.9 custom-call.28
  346.2 11.7 %cholesky.326 = f32[128,128]{1,0:T(8,128)S(1)} custom-call(f32[128,128]{1,0:T(8,128)S(1)} %cholesky.435), custom_call_target="Cholesky" | custom-call | tf_op jit(solution)/shard_map/jit(cholesky)/cholesky | solution.py:95
  358.0 9.8 custom-call.29
  368.6 11.9 %cholesky.343 = f32[128,128]{1,0:T(8,128)S(1)} custom-call(f32[128,128]{1,0:T(8,128)S(1)} %convolution_subtract_fusion.9), custom_call_target="Cholesky" | custom-call | tf_op jit(solution)/shard_map/jit(cholesky)/cholesky | solution.py:95
  385.4 8.3 while.8
  393.6 39.3 %custom-call.30 = f32[4,128,128]{1,2,0:T(8,128)S(1)} custom-call(f32[4,128,128]{2,1,0:T(8,128)S(1)} %get-tuple-element.61), custom_call_target="InvertDiagBlocksLowerTriangular" | custom-call | tf_op jit(solution)/shard_map/triangular_solve/custom-call.3 | solution.py:40
  433.0 2.4 fusion.44
  435.4 3.0 convolution_subtract_fusion.3
  439.6 3.5 convolution_subtract_fusion.1
  444.1 5.6 fusion.17
  451.7 2.6 broadcast_select_fusion.1
  454.3 122.6 %all-reduce.10.cloned.1.call-done = f32[2048,512]{0,1:T(8,128)} async-done(((f32[2048,512]{0,1:T(8,128)}), f32[2048,512]{0,1:T(8,128)}) %all-reduce.10.cloned.1.call-update) | async-done | bytes 4194320 | tf_op jit(solution)/shard_map/psum | solution.py:22
  579.3 50.9 %all-reduce.12.cloned.1.call-done = f32[512,512]{0,1:T(8,128)} async-done(((f32[512,512]{0,1:T(8,128)}), f32[512,512]{0,1:T(8,128)}) %all-reduce.12.cloned.1.call-update) | async-done | bytes 1048592 | tf_op jit(solution)/shard_map/psum | solution.py:103
  630.2 11.9 %subtract_select_fusion = f32[2048,512]{0,1:T(8,128)S(1)} fusion(f32[2048,512]{0,1:T(8,128)} %all-reduce.10.cloned.1.call-done, f32[2048,512]{0,1:T(8,128)} %copy.139, f32[512,512]{0,1:T(8,128)} %all-reduce.12.cloned.1.call-done, pred[]{:T(512)S(6)} %eq.46), kind=kOutput, calls=%fused_computation.14 | convolution fusion | flops 6444548096 | bytes 13631489 | tf_op jit(solution)/shard_map/dot_general | solution.py:104
  645.6 51.7 %all-reduce.14.cloned.1.call-done = f32[512,512]{0,1:T(8,128)} async-done(((f32[512,512]{0,1:T(8,128)}), f32[512,512]{0,1:T(8,128)}) %all-reduce.14.cloned.1.call-update) | async-done | bytes 1048592 | tf_op jit(solution)/shard_map/psum | solution.py:22
  700.3 11.7 %cholesky.358 = f32[128,128]{1,0:T(8,128)S(1)} custom-call(f32[128,128]{1,0:T(8,128)S(1)} %cholesky.439), custom_call_target="Cholesky" | custom-call | tf_op jit(solution)/shard_map/jit(cholesky)/cholesky | solution.py:95
  712.0 9.8 custom-call.31
  722.5 11.7 %cholesky.377 = f32[128,128]{1,0:T(8,128)S(1)} custom-call(f32[128,128]{1,0:T(8,128)S(1)} %cholesky.443), custom_call_target="Cholesky" | custom-call | tf_op jit(solution)/shard_map/jit(cholesky)/cholesky | solution.py:95
  734.6 10.2 custom-call.32
  745.9 11.7 %cholesky.398 = f32[128,128]{1,0:T(8,128)S(1)} custom-call(f32[128,128]{1,0:T(8,128)S(1)} %cholesky.448), custom_call_target="Cholesky" | custom-call | tf_op jit(solution)/shard_map/jit(cholesky)/cholesky | solution.py:95
  757.8 9.8 custom-call.33
  768.4 11.9 %cholesky.415 = f32[128,128]{1,0:T(8,128)S(1)} custom-call(f32[128,128]{1,0:T(8,128)S(1)} %convolution_subtract_fusion.8), custom_call_target="Cholesky" | custom-call | tf_op jit(solution)/shard_map/jit(cholesky)/cholesky | solution.py:95
  785.8 8.6 while.9
  794.4 39.3 %custom-call.34 = f32[4,128,128]{1,2,0:T(8,128)S(1)} custom-call(f32[4,128,128]{2,1,0:T(8,128)S(1)} %get-tuple-element.62), custom_call_target="InvertDiagBlocksLowerTriangular" | custom-call | tf_op jit(solution)/shard_map/triangular_solve/custom-call.3 | solution.py:40
  846.2 2.5 broadcast_select_fusion
  848.8 122.5 %all-reduce.16.cloned.1.call-done = f32[2048,512]{0,1:T(8,128)} async-done(((f32[2048,512]{0,1:T(8,128)}), f32[2048,512]{0,1:T(8,128)}) %all-reduce.16.cloned.1.call-update) | async-done | bytes 4194320 | tf_op jit(solution)/shard_map/psum | solution.py:22
  973.6 50.9 %all-reduce.18.cloned.1.call-done = f32[512,512]{0,1:T(8,128)} async-done(((f32[512,512]{0,1:T(8,128)}), f32[512,512]{0,1:T(8,128)}) %all-reduce.18.cloned.1.call-update) | async-done | bytes 1048592 | tf_op jit(solution)/shard_map/psum | solution.py:103
  1024.5 13.3 %select_bitcast_fusion = f32[1,2048,512]{1,2,0:T(8,128)} fusion(f32[2048,512]{0,1:T(8,128)} %all-reduce.16.cloned.1.call-done, f32[2048,512]{0,1:T(8,128)} %copy-done.1, f32[512,512]{0,1:T(8,128)} %all-reduce.18.cloned.1.call-done, pred[]{:T(512)S(6)} %eq.44, pred[2048]{0:T(1024)(128)(4,1)S(1)} %broadcast_compare_fusion.1, pred[512]{0:T(512)(128)(4,1)S(1)} %fusion.135), kind=kOutput, calls=%fused_computation.13 | convolution fusion | flops 6446645248 | bytes 13634049 | tf_op jit(solution)/shard_map/dot_general | solution.py:104
  1037.8 5.3 copy.164
  (186 shorter events, 75.6 us)
Async XLA Ops:
  6.5 4.8 copy-start.3
  11.3 3.4 copy-start.4
  12.5 25.7 %copy-start.6 = (s32[2]{0:T(128)S(1)}, s32[2]{0:T(128)}, u32[]{:S(2)}) copy-start(s32[2]{0:T(128)} %constant.461) | copy-start | bytes 28
  12.5 34.5 %collective-permute-start = (f32[64,4096]{1,0:T(8,128)}, f32[64,4096]{1,0:T(8,128)}, u32[]{:S(2)}, u32[]{:S(2)}) collective-permute-start(f32[64,4096]{1,0:T(8,128)} %get-tuple-element.124), channel_id=1, source_target_pairs={{0,64},{64,0},{128,192},{192,128},{1,65},{65,1},{129,193},{193,129... | collective-permute-start | bytes 3145736 | tf_op jit(solution)/shard_map/ppermute | solution.py:17
  30.3 8.7 copy-start.5
  120.4 101.2 %all-to-all-start = ((f32[128,16,512]{2,0,1:T(8,128)}), f32[128,16,512]{2,0,1:T(8,128)}, u32[]{:S(2)}, u32[]{:S(2)}) async-start(f32[128,16,512]{2,0,1:T(8,128)} %copy.138), calls=%async_computation | async-start | bytes 8388608 | tf_op jit(solution)/shard_map/all_to_all | solution.py:74
  127.3 170.4 %all-reduce.8.cloned.1.call-start = ((), (), s32[]{:S(2)}) async-start(), calls=%async_computation.1 | async-start | bytes 2097152 | tf_op jit(solution)/shard_map/psum | solution.py:22
  246.8 330.1 %all-reduce.10.cloned.1.call-start = ((), (), s32[]{:S(2)}) async-start(), calls=%async_computation.2 | async-start | bytes 8388608 | tf_op jit(solution)/shard_map/psum | solution.py:22
  433.0 6.6 copy-start
  454.3 175.9 %all-reduce.12.cloned.1.call-start = ((), (), s32[]{:S(2)}) async-start(), calls=%async_computation.3 | async-start | bytes 2097152 | tf_op jit(solution)/shard_map/psum | solution.py:103
  579.2 118.0 %all-reduce.14.cloned.1.call-start = ((), (), s32[]{:S(2)}) async-start(), calls=%async_computation.4 | async-start | bytes 2097152 | tf_op jit(solution)/shard_map/psum | solution.py:22
  642.1 2.0 copy-start.1
  645.3 325.9 %all-reduce.16.cloned.1.call-start = ((), (), s32[]{:S(2)}) async-start(), calls=%async_computation.5 | async-start | bytes 8388608 | tf_op jit(solution)/shard_map/psum | solution.py:22
  833.7 5.8 copy-start.2
  848.7 175.8 %all-reduce.18.cloned.1.call-start = ((), (), s32[]{:S(2)}) async-start(), calls=%async_computation.6 | async-start | bytes 2097152 | tf_op jit(solution)/shard_map/psum | solution.py:103
Sparse Core Ops, SparseCore 0:
  246.9 50.8 all-reduce.7
  454.4 122.4 all-reduce.9
  579.4 50.7 all-reduce.11
  645.4 51.7 all-reduce.13
  848.8 122.3 all-reduce.15
  973.7 50.7 all-reduce.17
where the time goes:
time: 1060 us; the launch traced here: 1050 us
  waiting for transfers between devices  540 us (51%)
  other arithmetic  334 us (32%)
  local copies, waits for them, and re-layouts  87.2 us (8%)
  matrix products  59.1 us (6%)
  between operations  19.6 us (2%)
    psum x4, waiting for transfers between devices, spread_2(): return lax.psum(block, axis)  347 us
    another operation x29, other arithmetic, on_device(): factor = jnp.linalg.cholesky(pivot_block)  158 us
    psum x2, waiting for transfers between devices, on_device(): lower_cols = lax.psum(col_pieces, 'row')  102 us
    all_to_all x1, waiting for transfers between devices, on_device(): lax.all_to_all(spread, 'col', split_axis=1, concat_axis=0, tiled=True)  90.6 us
    another operation x5, other arithmetic, solve_panel(): lax.linalg.triangular_solve(factor, rows_in, left_side=False, lower=True,...  78.9 us
    unnamed x4, other arithmetic  51.1 us
    another operation x14, matrix products, solve_panel(): lax.linalg.triangular_solve(factor, rows_in, left_side=False, lower=True,...  29.3 us
    dot_general x2, matrix products, on_device(): jnp.dot(lower_rows, lower_cols.T, precision=HIGHEST_PRECISION, preferred_...  25.2 us
  transfers between devices with their start and end apart: 8, of which 7 were waited for; matrix products, arithmetic and copies ran while one was open for 3% of the time, Pallas kernels for 0%

commit v1 on v0

--- a/solution.py
+++ b/solution.py
@@ -19,7 +19,7 @@
 
 def spread_2(block, axis, holder):
     block = jnp.where(lax.axis_index(axis) == holder, block, jnp.zeros_like(block))
-    return lax.psum(block, axis)
+    return jnp.sum(lax.all_gather(block, axis), axis=0)
 
 
 def storage_position(variable, parts, local_size):

time: 1060 us -> 1520 us (1.43)
  waiting for transfers between devices: 540 us -> 957 us
  other arithmetic: 334 us -> 385 us
    all_gather x0 -> x4, waiting for transfers between devices: none -> 768 us  [spread_2(): return jnp.sum(lax.all_gather(block, axis), axis=0)]
    psum x4 -> x0, waiting for transfers between devices: 347 us -> none  [spread_2(): return lax.psum(block, axis)]
    reduce_sum x0 -> x4, other arithmetic: none -> 51.7 us  [spread_2(): return jnp.sum(lax.all_gather(block, axis), axis=0)]
  transfers between devices with their start and end apart: 8 -> 8, of which waited for: 7 -> 7; matrix products, arithmetic and copies ran while one was open for 3% -> 2% of each run, Pallas kernels for 0% -> 0%
where the time goes in v1:
time: 1520 us; the launch traced here: 1510 us
  waiting for transfers between devices  957 us (63%)
  other arithmetic  385 us (25%)
  local copies, waits for them, and re-layouts  73.1 us (5%)
  matrix products  64.4 us (4%)
  between operations  19.5 us (1%)
    all_gather x4, waiting for transfers between devices, spread_2(): return jnp.sum(lax.all_gather(block, axis), axis=0)  768 us
    another operation x29, other arithmetic, on_device(): factor = jnp.linalg.cholesky(pivot_block)  159 us
    psum x2, waiting for transfers between devices, on_device(): lower_cols = lax.psum(col_pieces, 'row')  99.1 us
    all_to_all x1, waiting for transfers between devices, on_device(): lax.all_to_all(spread, 'col', split_axis=1, concat_axis=0, tiled=True)  90.6 us
    another operation x5, other arithmetic, solve_panel(): lax.linalg.triangular_solve(factor, rows_in, left_side=False, lower=True,...  78.9 us
    reduce_sum x4, other arithmetic, spread_2(): return jnp.sum(lax.all_gather(block, axis), axis=0)  51.7 us
    unnamed x4, other arithmetic  51.1 us
    another operation x14, matrix products, solve_panel(): lax.linalg.triangular_solve(factor, rows_in, left_side=False, lower=True,...  36 us
  transfers between devices with their start and end apart: 8, of which 7 were waited for; matrix products, arithmetic and copies ran while one was open for 2% of the time, Pallas kernels for 0%

profile of v1, /device:TPU:8, one launch (start us, length us, event | category | flops | bytes accessed | tf_op | source)
XLA Modules:
  0.0 1510.0 jit_solution(15141569457162950772)
XLA Ops:
  6.5 4.8 copy.176
  16.2 14.1 gather_fusion.1
  30.3 7.2 compare_select_fusion
  51.3 48.2 %scatter_custom_fusion.1 = f32[16384,64]{1,0:T(8,128)} fusion(s32[8192]{0:T(1024)S(1)} %bitcast.182, f32[8192,64]{1,0:T(8,128)} %bitcast.175, f32[]{:T(128)} %constant.447.clone.1), kind=kCustom, calls=%fused_computation.11 | custom fusion | flops 524288 | bytes 4194816
  99.5 8.7 copy.130
  108.1 4.6 copy.105
  112.8 3.3 copy.135
  116.0 4.4 copy.106
  120.4 6.9 all-to-all-start
  127.6 2.8 gather_fusion
  131.0 90.6 %all-to-all-done = f32[128,16,512]{2,0,1:T(8,128)} async-done(((f32[128,16,512]{2,0,1:T(8,128)}), f32[128,16,512]{2,0,1:T(8,128)}, u32[]{:S(2)}, u32[]{:S(2)}) %all-to-all-start) | async-done | bytes 4194336 | tf_op jit(solution)/shard_map/all_to_all | solution.py:74
  221.6 17.4 %scatter_fusion = f32[2048,512]{1,0:T(8,128)} fusion(f32[2048,512]{1,0:T(8,128)} %bitcast.164, s32[2048]{0:T(1024)S(1)} %bitcast.181, f32[2048,512]{1,0:T(8,128)} %bitcast.19), kind=kCustom, calls=%fused_computation.2 | custom fusion | flops 1048576 | bytes 12591104 | tf_op jit(solution)/shard_map/scatter-add | solution.py:82
  241.9 50.4 %all-gather.9.cloned.1.call-done = f32[2048,512]{1,0:T(8,128)} async-done(((f32[512,512]{1,0:T(8,128)}), f32[2048,512]{1,0:T(8,128)}) %all-gather.9.cloned.1.call-update) | async-done | bytes 4194320 | tf_op jit(solution)/shard_map/all_gather | solution.py:22
  292.2 2.8 reduce_sum.36
  295.6 11.7 cholesky.286
  307.5 9.8 custom-call.27
  318.0 11.7 cholesky.305
  329.7 10.0 custom-call.28
  340.3 11.7 cholesky.326
  352.8 9.8 custom-call.29
  363.2 12.1 cholesky.343
  379.4 8.1 while.8
  387.6 39.3 %custom-call.30 = f32[4,128,128]{1,2,0:T(8,128)S(1)} custom-call(f32[4,128,128]{2,1,0:T(8,128)S(1)} %get-tuple-element.61), custom_call_target="InvertDiagBlocksLowerTriangular" | custom-call | tf_op jit(solution)/shard_map/triangular_solve/custom-call.3 | solution.py:40
  429.2 4.1 convolution_subtract_fusion.3
  435.8 3.2 convolution_subtract_fusion.1
  439.9 4.3 fusion.17
  449.7 332.7 %all-gather.11.cloned.1.call-done = f32[32768,512]{1,0:T(8,128)} async-done(((f32[2048,512]{1,0:T(8,128)}), f32[32768,512]{1,0:T(8,128)}) %all-gather.11.cloned.1.call-update) | async-done | bytes 67108880 | tf_op jit(solution)/shard_map/all_gather | solution.py:22
  782.4 23.1 %reduce_sum.37 = f32[2048,512]{1,0:T(8,128)} reduce(f32[16,2048,512]{2,1,0:T(8,128)} %bitcast.33, f32[]{:T(128)} %constant.447.clone.1), dimensions={0}, to_apply=%region_11.14 | reduce | flops 15728640 | bytes 71303168 | tf_op jit(solution)/shard_map/reduce_sum | solution.py:22
  807.9 49.5 %all-reduce.4.cloned.1.call-done = f32[512,512]{1,0:T(8,128)} async-done(((f32[512,512]{1,0:T(8,128)}), f32[512,512]{1,0:T(8,128)}) %all-reduce.4.cloned.1.call-update) | async-done | bytes 1048592 | tf_op jit(solution)/shard_map/psum | solution.py:103
  857.5 11.7 subtract_select_fusion
  872.4 51.8 %all-gather.13.cloned.1.call-done = f32[2048,512]{1,0:T(8,128)} async-done(((f32[512,512]{1,0:T(8,128)}), f32[2048,512]{1,0:T(8,128)}) %all-gather.13.cloned.1.call-update) | async-done | bytes 4194320 | tf_op jit(solution)/shard_map/all_gather | solution.py:22
  924.2 2.8 reduce_sum.38
  927.6 11.7 cholesky.358
  939.5 9.8 custom-call.31
  949.9 11.7 cholesky.377
  963.0 10.2 custom-call.32
  973.9 11.7 cholesky.398
  986.3 9.8 custom-call.33
  996.7 11.8 cholesky.415
  1012.0 8.1 while.9
  1020.2 39.3 %custom-call.34 = f32[4,128,128]{1,2,0:T(8,128)S(1)} custom-call(f32[4,128,128]{2,1,0:T(8,128)S(1)} %get-tuple-element.62), custom_call_target="InvertDiagBlocksLowerTriangular" | custom-call | tf_op jit(solution)/shard_map/triangular_solve/custom-call.3 | solution.py:40
  1061.8 4.1 convolution_subtract_fusion.2
  1068.4 3.2 convolution_subtract_fusion
  1072.6 4.3 fusion.14
  1082.3 332.7 %all-gather.15.cloned.1.call-done = f32[32768,512]{1,0:T(8,128)} async-done(((f32[2048,512]{1,0:T(8,128)}), f32[32768,512]{1,0:T(8,128)}) %all-gather.15.cloned.1.call-update) | async-done | bytes 67108880 | tf_op jit(solution)/shard_map/all_gather | solution.py:22
  1415.0 23.1 %reduce_sum.39 = f32[2048,512]{1,0:T(8,128)} reduce(f32[16,2048,512]{2,1,0:T(8,128)} %bitcast.47, f32[]{:T(128)} %constant.447.clone.1), dimensions={0}, to_apply=%region_14.17 | reduce | flops 15728640 | bytes 71303168 | tf_op jit(solution)/shard_map/reduce_sum | solution.py:22
  1440.5 49.5 %all-reduce.6.cloned.1.call-done = f32[512,512]{1,0:T(8,128)} async-done(((f32[512,512]{1,0:T(8,128)}), f32[512,512]{1,0:T(8,128)}) %all-reduce.6.cloned.1.call-update) | async-done | bytes 1048592 | tf_op jit(solution)/shard_map/psum | solution.py:103
  1490.1 12.9 select_bitcast_fusion
  (156 shorter events, 79.1 us)
Async XLA Ops:
  6.5 4.8 copy-start.3
  11.3 3.4 copy-start.4
  12.5 25.7 %copy-start.6 = (s32[2]{0:T(128)S(1)}, s32[2]{0:T(128)}, u32[]{:S(2)}) copy-start(s32[2]{0:T(128)} %constant.461) | copy-start | bytes 28
  12.5 34.5 %collective-permute-start = (f32[64,4096]{1,0:T(8,128)}, f32[64,4096]{1,0:T(8,128)}, u32[]{:S(2)}, u32[]{:S(2)}) collective-permute-start(f32[64,4096]{1,0:T(8,128)} %get-tuple-element.84), channel_id=1, source_target_pairs={{0,64},{64,0},{128,192},{192,128},{1,65},{65,1},{129,193},{193,129... | collective-permute-start | bytes 3145736 | tf_op jit(solution)/shard_map/ppermute | solution.py:17
  30.3 8.7 copy-start.5
  120.4 101.2 %all-to-all-start = ((f32[128,16,512]{2,0,1:T(8,128)}), f32[128,16,512]{2,0,1:T(8,128)}, u32[]{:S(2)}, u32[]{:S(2)}) async-start(f32[128,16,512]{2,0,1:T(8,128)} %copy.106), calls=%async_computation | async-start | bytes 8388608 | tf_op jit(solution)/shard_map/all_to_all | solution.py:74
  127.3 164.9 %all-gather.9.cloned.1.call-start = ((), (), s32[]{:S(2)}) async-start(), calls=%async_computation.3 | async-start | bytes 5242880 | tf_op jit(solution)/shard_map/all_gather | solution.py:22
  241.4 541.0 %all-gather.11.cloned.1.call-start = ((), (), s32[]{:S(2)}) async-start(), calls=%async_computation.4 | async-start | bytes 71303168 | tf_op jit(solution)/shard_map/all_gather | solution.py:22
  387.5 41.6 %copy-start.1 = (f32[512,512]{1,0:T(8,128)}, f32[512,512]{1,0:T(8,128)S(1)}, u32[]{:S(2)}) copy-start(f32[512,512]{1,0:T(8,128)S(1)} %get-tuple-element.225) | copy-start | bytes 3145732
  449.4 408.0 %all-reduce.4.cloned.1.call-start = ((), (), s32[]{:S(2)}) async-start(), calls=%async_computation.1 | async-start | bytes 2097152 | tf_op jit(solution)/shard_map/psum | solution.py:103
  807.9 116.3 %all-gather.13.cloned.1.call-start = ((), (), s32[]{:S(2)}) async-start(), calls=%async_computation.5 | async-start | bytes 5242880 | tf_op jit(solution)/shard_map/all_gather | solution.py:22
  869.2 2.0 copy-start
  872.4 542.7 %all-gather.15.cloned.1.call-start = ((), (), s32[]{:S(2)}) async-start(), calls=%async_computation.6 | async-start | bytes 71303168 | tf_op jit(solution)/shard_map/all_gather | solution.py:22
  1020.2 41.6 %copy-start.2 = (f32[512,512]{1,0:T(8,128)}, f32[512,512]{1,0:T(8,128)S(1)}, u32[]{:S(2)}) copy-start(f32[512,512]{1,0:T(8,128)S(1)} %get-tuple-element.226) | copy-start | bytes 3145732
  1082.1 408.0 %all-reduce.6.cloned.1.call-start = ((), (), s32[]{:S(2)}) async-start(), calls=%async_computation.2 | async-start | bytes 2097152 | tf_op jit(solution)/shard_map/psum | solution.py:103
Sparse Core Ops, SparseCore 0:
  241.5 50.6 all-gather.8
  449.6 332.8 all-gather.10
  808.0 49.4 all-reduce.3
  872.5 51.6 all-gather.12
  1082.2 332.8 all-gather.14
  1440.6 49.4 all-reduce.5
